TPU v7x, 128 devices: a whole 4x4x4 slice. The times are simulated.
128 devices in a mesh: head: 4 (over z_lo, core), tok: 32 (over x, z_hi, y).
Axes of the slice: x: 4, y: 4, z: 4 (z_hi: 2, z_lo: 2; z = z_hi * 2 + z_lo), core: 2. Of those that a mesh axis runs over, the one named last changes fastest.
Arguments:
- hidden_in: bfloat16 [8192, 2048], P('tok'), may hold values from -6 to 6
- queries: bfloat16 [8192, 2048], P('tok', 'head'), may hold values from -4.5 to 4.5
- keys: bfloat16 [8192, 2048], P('tok', 'head'), may hold values from -4.5 to 4.5
- values: bfloat16 [8192, 2048], P('tok', 'head'), may hold values from -6 to 6
- request_ids: int32 [8192], replicated, may hold values from 0 to 63, never falling along the last dimension, each value on 1 to 1024 neighbouring positions
- out_proj: bfloat16 [2048, 2048], P('head'), may hold values from -0.125 to 0.125
- norm_gain: float32 [2048], replicated, may hold values from 0.1 to 1.9
- expert_gate_up: bfloat16 [32, 2048, 2, 1408], P('tok', None, None, 'head'), may hold values from -0.125 to 0.125
- expert_down: bfloat16 [32, 1408, 2048], P('tok', 'head'), may hold values from -0.15625 to 0.15625
- shared_gate_up: bfloat16 [2048, 2, 2816], P(None, None, 'head'), may hold values from -0.125 to 0.125
- shared_down: bfloat16 [2816, 2048], P('head'), may hold values from -0.109375 to 0.109375
- shared_gate: bfloat16 [2048], replicated, may hold values from -0.125 to 0.125
- routes: int32 [8192, 4], P('tok'), may hold values from 0 to 31, all different within a row; in each aligned block of 256 rows (0 to 255, 256 to 511, ...) at most 48 rows name the same one
- route_weights: float32 [8192, 4], P('tok'), may hold values from 0.05 to 0.5
- page_slots: int32 [1024], replicated, may hold values from 0 to 1023, as said below
Outputs:
- layer_out: bfloat16 [8192, 2048], P('tok', 'head')
- decode_cache: bfloat16 [1024, 8, 4096], P('tok', 'head')
Inputs may be any that keep to these rules, and one draw needn't show every extreme that they name: `request_ids`: ids never fall along the tokens; each request holds 1 to 1024 consecutive tokens, and one holds exactly 1024. `routes`: each row names 4 different experts; among the rows of one device no expert is named more than 48 times, a bound that some block reaches. `page_slots`: a permutation; for any two aligned blocks, one of 32 pages and one of 32 cache rows, the number of pages of the first that go to rows of the second is exactly 1.
All inputs are finite; a program needn't handle non-finite values.
Results may differ from a plain program's by a relative error of at most 0.0065.
Values may be sent and summed in bfloat16 or wider, within the bound.
No kernel may reach another device: no remote copies, remote signals or barrier semaphores. Data moves between devices by JAX's collectives and lax.ppermute only.
A program may use at most 128 MiB of HBM per device.

v0:
```python
import math
import jax
import jax.numpy as jnp
from jax import lax
from jax.sharding import PartitionSpec as P

HD = 128
TOP = 4
EXPERTS = 32
PAGE = 8
REACH = 4
CAP = 48


def from_behind(value, axis, steps):
    count = lax.axis_size(axis)
    leading, last = (max(0, -steps), min(count, count - steps))
    return lax.ppermute(value, axis, [(source, source + steps) for source in range(leading, last)])


def run_experts(slots, gate_up, down):
    both = jnp.einsum("secd,edgf->secgf", slots, gate_up, preferred_element_type=jnp.float32)
    active = (jax.nn.silu(both[..., 0, :]) * both[..., 1, :]).astype(jnp.bfloat16)
    return jnp.einsum("secf,efd->secd", active, down, preferred_element_type=jnp.float32)


def per_device(
    hidden_in,
    queries,
    keys,
    values,
    request_ids,
    out_proj,
    norm_gain,
    expert_gate_up,
    expert_down,
    shared_gate_up,
    shared_down,
    shared_gate,
    routes,
    route_weights,
    page_slots,
):
    tok_rows = hidden_in.shape[0]
    model_width = hidden_in.shape[1]
    head_width = queries.shape[1]
    heads_here = head_width // HD
    tok_count = lax.axis_size("tok")
    head_count = lax.axis_size("head")
    tok_index = lax.axis_index("tok")
    head_index = lax.axis_index("head")
    column_width = model_width // head_count
    key_list = [keys]
    value_list = [values]
    for step in range(1, REACH + 1):
        far_keys, far_values = from_behind((keys, values), "tok", step)
        key_list.insert(0, far_keys)
        value_list.insert(0, far_values)
    span = REACH * tok_rows
    window_keys = jnp.concatenate(key_list, 0).reshape(span + tok_rows, heads_here, HD)
    window_values = jnp.concatenate(value_list, 0).reshape(span + tok_rows, heads_here, HD)
    padded_ids = jnp.concatenate([jnp.full((span,), -1, jnp.int32), request_ids], 0)
    base = tok_index * tok_rows
    key_ids = lax.dynamic_slice_in_dim(padded_ids, base, span + tok_rows, 0)
    query_ids = lax.dynamic_slice_in_dim(request_ids, base, tok_rows, 0)
    query_pos = jnp.arange(tok_rows, dtype=jnp.int32) + span
    key_pos = jnp.arange(span + tok_rows, dtype=jnp.int32)
    allowed = (query_ids[:, None] == key_ids[None, :]) & (key_pos[None, :] <= query_pos[:, None])
    scores = jnp.einsum(
        "qhd,khd->hqk",
        queries.reshape(tok_rows, heads_here, HD),
        window_keys,
        preferred_element_type=jnp.float32,
    ) * (1.0 / math.sqrt(HD))
    scores = jnp.where(allowed[None], scores, -1e30)
    top = jnp.max(scores, axis=-1, keepdims=True)
    weights = jnp.exp(scores - top)
    probs = (weights / jnp.sum(weights, axis=-1, keepdims=True)).astype(jnp.bfloat16)
    attended = (
        jnp.einsum("hqk,khd->qhd", probs, window_values, preferred_element_type=jnp.float32)
        .astype(jnp.bfloat16)
        .reshape(tok_rows, head_width)
    )
    projected = jnp.dot(attended, out_proj, preferred_element_type=jnp.float32)
    total = lax.psum(projected, "head")
    resid = hidden_in.astype(jnp.float32) + total
    mean_square = jnp.mean(resid * resid, axis=-1, keepdims=True)
    normed = (resid * lax.rsqrt(mean_square + 1e-06) * norm_gain).astype(jnp.bfloat16)
    resid_cols = lax.dynamic_slice_in_dim(resid, head_index * column_width, column_width, 1)
    shared_both = jnp.einsum(
        "td,dgf->tgf", normed, shared_gate_up, preferred_element_type=jnp.float32
    )
    shared_act = (jax.nn.silu(shared_both[:, 0, :]) * shared_both[:, 1, :]).astype(jnp.bfloat16)
    shared_scale = jax.nn.sigmoid(jnp.dot(normed, shared_gate, preferred_element_type=jnp.float32))
    shared_term = shared_scale[:, None] * jnp.dot(
        shared_act, shared_down, preferred_element_type=jnp.float32
    )
    flat_routes = routes.reshape(-1)
    assign = tok_rows * TOP
    expert_ids = jnp.arange(EXPERTS, dtype=jnp.int32)
    onehot = (flat_routes[:, None] == expert_ids[None, :]).astype(jnp.int32)
    before = jnp.cumsum(onehot, 0) - onehot
    rank = jnp.sum(before * onehot, 1)
    slot = flat_routes * CAP + rank
    source_row = (
        jnp.zeros((EXPERTS * CAP,), jnp.int32)
        .at[slot]
        .set(jnp.arange(assign, dtype=jnp.int32) // TOP)
    )
    filled = jnp.zeros((EXPERTS * CAP,), jnp.bool_).at[slot].set(True)
    outgoing = jnp.where(filled[:, None], normed[source_row], jnp.zeros((), jnp.bfloat16))
    local_experts = EXPERTS // tok_count
    outgoing = outgoing.reshape(tok_count, local_experts, CAP, model_width)
    partial_value = run_experts(
        lax.all_to_all(outgoing, "tok", split_axis=0, concat_axis=0, tiled=True),
        expert_gate_up,
        expert_down,
    )
    flat_weights = route_weights.reshape(tok_rows, TOP, 1)
    slot_cols, shared_cols = (
        lax.psum_scatter(
            partial_value.reshape(EXPERTS * CAP, model_width),
            "head",
            scatter_dimension=1,
            tiled=True,
        ),
        lax.psum_scatter(shared_term, "head", scatter_dimension=1, tiled=True),
    )
    returned = lax.all_to_all(
        slot_cols.reshape(tok_count, local_experts * CAP, column_width).astype(jnp.bfloat16),
        "tok",
        split_axis=0,
        concat_axis=0,
        tiled=True,
    ).astype(jnp.float32)
    picked = returned.reshape(EXPERTS * CAP, column_width)[slot].reshape(
        tok_rows, TOP, column_width
    )
    moe_cols = jnp.sum(picked * flat_weights, 1)
    layer_cols = resid_cols + shared_cols + moe_cols
    layer_out = layer_cols.astype(jnp.bfloat16)
    pages_here = tok_rows // PAGE
    pair = pages_here // tok_count
    quarter_page = PAGE // head_count
    slots_all = page_slots.reshape(tok_count, pages_here)
    owner_all = slots_all // pages_here
    same_owner = owner_all[:, :, None] == owner_all[:, None, :]
    earlier = slots_all[:, None, :] < slots_all[:, :, None]
    rank_all = jnp.sum((same_owner & earlier).astype(jnp.int32), 2)
    send_pos = owner_all * pair + rank_all
    mine_pos = lax.dynamic_index_in_dim(send_pos, tok_index, 0, keepdims=False)
    page_ids = jnp.arange(pages_here, dtype=jnp.int32)
    send_order = jnp.zeros((pages_here,), jnp.int32).at[mine_pos].set(page_ids)
    sources = jnp.arange(tok_count, dtype=jnp.int32)[:, None]
    target = jnp.where(owner_all == tok_index, sources * pair + rank_all, pages_here)
    arrival_slot = (
        jnp.zeros((pages_here + 1,), jnp.int32)
        .at[target.reshape(-1)]
        .set((slots_all % pages_here).reshape(-1))[:pages_here]
    )
    place_order = jnp.zeros((pages_here,), jnp.int32).at[arrival_slot].set(page_ids)
    kv_pages = jnp.stack([keys, values], 1).reshape(
        pages_here, head_count, quarter_page, 2, heads_here, HD
    )[send_order]
    row_width = 2 * head_count * heads_here * HD
    spread = kv_pages.reshape(
        tok_count, pair, head_count, quarter_page, 2, heads_here, HD
    ).transpose(2, 0, 1, 3, 4, 5, 6)
    spread = spread.reshape(head_count * tok_count, pair, quarter_page, 2, heads_here, HD)
    landed = lax.all_to_all(spread, ("head", "tok"), split_axis=0, concat_axis=0, tiled=True)
    landed = landed.reshape(head_count, tok_count, pair, quarter_page, 2, heads_here, HD).transpose(
        1, 2, 3, 4, 0, 5, 6
    )
    landed = landed.reshape(pages_here, quarter_page, row_width)
    decode_cache = landed[place_order]
    return (layer_out, decode_cache)


def solution(mesh):
    in_specs = (
        P("tok", None),
        P("tok", "head"),
        P("tok", "head"),
        P("tok", "head"),
        P(),
        P("head", None),
        P(),
        P("tok", None, None, "head"),
        P("tok", "head", None),
        P(None, None, "head"),
        P("head", None),
        P(),
        P("tok", None),
        P("tok", None),
        P(),
    )
    out_specs = (P("tok", "head"), P("tok", "head", None))
    return jax.shard_map(
        per_device, mesh=mesh, in_specs=in_specs, out_specs=out_specs, check_vma=False
    )
```

profile of v0, /device:TPU:8, one launch (start us, length us, event | category | flops | bytes accessed | tf_op | source)
XLA Modules:
  0.0 430.8 jit_solution(11822778492569103594)
XLA Ops:
  8.5 5.8 %collective-permute-start.4 = (bf16[256,512]{0,1:T(8,128)(2,1)S(1)}, bf16[256,512]{0,1:T(8,128)(2,1)S(1)}, u32[]{:S(2)}, u32[]{:S(2)}) collective-permute-start(bf16[256,512]{0,1:T(8,128)(2,1)S(1)} %copy.77), channel_id=1, source_target_pairs={{0,4},{1,5},{2,6},{3,7},{4,8},{5,9},{6,10},{7,11},{8,12},{9,13},{1... | collective-permute-start | bytes 786440 | tf_op jit(solution)/shard_map/ppermute | solution.py:18
  14.3 3.1 collective-permute-start.5
  17.3 4.5 %collective-permute-start.6 = (bf16[256,512]{0,1:T(8,128)(2,1)S(1)}, bf16[256,512]{0,1:T(8,128)(2,1)}, u32[]{:S(2)}, u32[]{:S(2)}) collective-permute-start(bf16[256,512]{0,1:T(8,128)(2,1)S(1)} %copy.77), channel_id=1, source_target_pairs={{0,2},{1,3},{2,4},{3,5},{4,6},{5,7},{6,8},{7,9},{8,10},{9,11},{10,... | collective-permute-start | bytes 786440 | tf_op jit(solution)/shard_map/ppermute | solution.py:18
  21.8 3.1 collective-permute-start.7
  25.0 6.5 %collective-permute-start = (bf16[256,512]{1,0:T(8,128)(2,1)}, bf16[256,512]{1,0:T(8,128)(2,1)}, u32[]{:S(2)}, u32[]{:S(2)}) collective-permute-start(bf16[256,512]{1,0:T(8,128)(2,1)} %param.18), channel_id=1, source_target_pairs={{0,4},{1,5},{2,6},{3,7},{4,8},{5,9},{6,10},{7,11},{8,12},{9,13},{1... | collective-permute-start | bytes 786440 | tf_op jit(solution)/shard_map/ppermute | solution.py:18
  34.0 9.6 %collective-permute-start.1 = (bf16[256,512]{1,0:T(8,128)(2,1)}, bf16[256,512]{1,0:T(8,128)(2,1)S(1)}, u32[]{:S(2)}, u32[]{:S(2)}) collective-permute-start(bf16[256,512]{1,0:T(8,128)(2,1)} %param.18), channel_id=1, source_target_pairs={{0,3},{1,4},{2,5},{3,6},{4,7},{5,8},{6,9},{7,10},{8,11},{9,12},{10... | collective-permute-start | bytes 786440 | tf_op jit(solution)/shard_map/ppermute | solution.py:18
  46.1 4.0 collective-permute-start.3
  56.9 2.4 copy.76
  59.3 3.5 exponential_reduce_fusion
  62.8 4.5 %fusion.15 = bf16[4,128,256]{2,1,0:T(8,128)(2,1)S(1)} fusion(bf16[1280,4,128]{0,2,1:T(8,128)(2,1)} %bitcast.151, f32[4,256]{1,0:T(4,128)S(1)} %exponential_reduce_fusion, bf16[1280,4,128]{0,2,1:T(8,128)(2,1)} %bitcast.155, pred[256,1280]{0,1:T(8,128)(4,1)} %fusion.14, bf16[256,512]{1,0:T(8,128)(2,1)} %param.16), kind=kOutput, calls=%fused_computation.32 | convolution fusion | flops 677775616 | bytes 3477504 | tf_op jit(solution)/shard_map/hqk,khd->qhd/dot_general | solution.py:80
  67.3 3.6 fusion.75
  72.0 9.0 %reduce-window.6 = s32[32,8,128]{2,1,0:T(8,128)S(1)} reduce-window(s32[32,8,128]{2,1,0:T(8,128)S(1)} %fusion.42, s32[]{:T(128)} %constant.46.clone.1), window={size=1x1x128 pad=0_0x0_0x127_0}, to_apply=%region_5.6 | reduce-window | flops 4161536 | bytes 262148 | tf_op jit(solution)/shard_map/reduce-window
  81.8 4.5 %scatter_custom_fusion.1 = s32[1536]{0:T(1024)S(1)} fusion(s32[1024]{0:T(1024)S(1)} %bitcast.158, s32[1024]{0:T(1024)S(1)} %add_select_fusion.3, s32[]{:T(128)} %constant.46.clone.1), kind=kCustom, calls=%fused_computation.98 | custom fusion | bytes 6148 | tf_op jit(solution)/shard_map/scatter | solution.py:108
  86.3 4.3 %scatter_custom_fusion = pred[1536]{0:T(1024)(128)(4,1)S(1)} fusion(s32[1024]{0:T(1024)S(1)} %bitcast.159, pred[1024]{0:T(1024)(128)(4,1)S(1)} %broadcast.250, pred[]{:T(512)} %constant.99.clone.1), kind=kCustom, calls=%fused_computation.102 | custom fusion | bytes 1537 | tf_op jit(solution)/shard_map/scatter | solution.py:110
  90.8 46.8 %all-reduce.3.cloned.1.call-done = f32[256,2048]{1,0:T(8,128)} async-done(((f32[256,2048]{1,0:T(8,128)}), f32[256,2048]{1,0:T(8,128)}) %all-reduce.3.cloned.1.call-update) | async-done | bytes 2097168 | tf_op jit(solution)/shard_map/psum | solution.py:85
  142.3 14.1 %gather_fusion = bf16[1536,2048]{1,0:T(8,128)(2,1)} fusion(bf16[256,2048]{1,0:T(8,128)(2,1)} %multiply_convert_fusion, s32[2048]{0:T(1024)S(1)} %pad_clamp_fusion), kind=kCustom, calls=%fused_computation | custom fusion | bytes 12589056 | tf_op jit(solution)/shard_map/gather | solution.py:111
  156.4 3.3 broadcast_select_fusion
  159.7 83.4 %all_to_all.15 = bf16[32,1,48,2048]{3,2,1,0:T(8,128)(2,1)S(1)} all-to-all(bf16[32,1,48,2048]{3,2,1,0:T(8,128)(2,1)S(1)} %broadcast_select_fusion), channel_id=1, replica_groups=mesh['head'=4,'tok'=32] {'tok'}, dimensions={0} | all-to-all | bytes 12582912 | tf_op jit(solution)/shard_map/all_to_all | solution.py:115
  243.1 5.2 %fusion.7 = f32[32,1,48,2,352]{4,2,3,0,1:T(8,128)S(1)} fusion(bf16[1,2048,2,352]{1,3,2,0:T(8,128)(2,1)S(1)} %copy-done, bf16[32,1,48,2048]{3,2,1,0:T(8,128)(2,1)S(1)} %all_to_all.15), kind=kOutput, calls=%fused_computation.22 | convolution fusion | flops 4429185024 | bytes 13500416 | tf_op jit(solution)/shard_map/secd,edgf->secgf/dot_general | solution.py:22
  248.3 6.4 %fusion.12 = f32[32,48,2048]{2,1,0:T(8,128)} fusion(bf16[1,352,2048]{2,1,0:T(8,128)(2,1)S(1)} %copy-done.13, f32[32,1,48,2,352]{4,2,3,0,1:T(8,128)S(1)} %fusion.7), kind=kOutput, calls=%fused_computation.28 | convolution fusion | flops 2217836544 | bytes 18350080 | tf_op jit(solution)/shard_map/secf,efd->secd/dot_general | solution.py:24
  256.4 4.5 %fusion.18 = f32[256,2,704]{0,2,1:T(8,128)S(1)} fusion(bf16[2048,2,704]{0,2,1:T(8,128)(2,1)} %param.24, bf16[256,2048]{1,0:T(8,128)(2,1)S(1)} %copy-done.2), kind=kOutput, calls=%fused_computation.34 | convolution fusion | flops 1476395008 | bytes 8257536 | tf_op jit(solution)/shard_map/td,dgf->tgf/dot_general | solution.py:90
  260.9 2.4 convolution_multiply_fusion
  265.2 4.3 scatter_custom_fusion.3
  273.5 4.5 %all-to-all-start.2 = ((bf16[128,1,2,2,4,128]{5,4,3,2,1,0:T(4,128)(2,1)}), bf16[128,1,2,2,4,128]{5,4,3,2,1,0:T(4,128)(2,1)S(1)}, u32[]{:S(2)}, u32[]{:S(2)}) async-start(bf16[128,1,2,2,4,128]{5,4,3,2,1,0:T(4,128)(2,1)} %copy.93), calls=%async_computation.4 | async-start | bytes 1048576 | tf_op jit(solution)/shard_map/all_to_all | solution.py:170
  278.0 92.0 %reduce-scatter.5.cloned.1.call-done = f32[1536,512]{1,0:T(8,128)} async-done(((f32[1536,2048]{1,0:T(8,128)}), f32[1536,512]{1,0:T(8,128)}) %reduce-scatter.5.cloned.1.call-update) | async-done | bytes 3145744 | tf_op jit(solution)/shard_map/reduce_scatter | solution.py:121
  370.0 3.2 convert_element_type.57
  373.3 9.8 %all-to-all-start.1 = ((bf16[32,48,512]{2,1,0:T(8,128)(2,1)}), bf16[32,48,512]{2,1,0:T(8,128)(2,1)S(1)}, u32[]{:S(2)}, u32[]{:S(2)}) async-start(bf16[32,48,512]{2,1,0:T(8,128)(2,1)} %bitcast.32), calls=%async_computation.3 | async-start | bytes 3145728 | tf_op jit(solution)/shard_map/all_to_all | solution.py:129
  384.4 2.4 gather_fusion.3
  386.8 20.0 %all-to-all-done.1 = bf16[32,48,512]{2,1,0:T(8,128)(2,1)S(1)} async-done(((bf16[32,48,512]{2,1,0:T(8,128)(2,1)}), bf16[32,48,512]{2,1,0:T(8,128)(2,1)S(1)}, u32[]{:S(2)}, u32[]{:S(2)}) %all-to-all-start.1) | async-done | bytes 1572896 | tf_op jit(solution)/shard_map/all_to_all | solution.py:129
  409.0 7.2 %gather_fusion.1 = f32[1024,512]{1,0:T(8,128)} fusion(f32[1536,512]{1,0:T(8,128)} %bitcast_convert_fusion, s32[1024]{0:T(1024)S(1)} %broadcast_clamp_fusion), kind=kCustom, calls=%fused_computation.1 | custom fusion | bytes 4198400 | tf_op jit(solution)/shard_map/gather | solution.py:136
  416.2 3.1 reshape.311
  419.3 2.9 multiply_reduce_fusion
  (116 shorter events, 32.6 us)
Async XLA Ops:
  7.2 236.0 %copy-start = (bf16[1,2048,2,352]{1,3,2,0:T(8,128)(2,1)S(1)}, bf16[1,2048,2,352]{1,3,2,0:T(8,128)(2,1)}, u32[]{:S(2)}) copy-start(bf16[1,2048,2,352]{1,3,2,0:T(8,128)(2,1)} %param.22) | copy-start | bytes 8650756
  7.2 130.4 %all-reduce.3.cloned.1.call-start = ((), (), s32[]{:S(2)}) async-start(), calls=%async_computation.5 | async-start | bytes 4194304 | tf_op jit(solution)/shard_map/psum | solution.py:85
  8.5 25.6 %collective-permute-start.4 = (bf16[256,512]{0,1:T(8,128)(2,1)S(1)}, bf16[256,512]{0,1:T(8,128)(2,1)S(1)}, u32[]{:S(2)}, u32[]{:S(2)}) collective-permute-start(bf16[256,512]{0,1:T(8,128)(2,1)S(1)} %copy.77), channel_id=1, source_target_pairs={{0,4},{1,5},{2,6},{3,7},{4,8},{5,9},{6,10},{7,11},{8,12},{9,13},{1... | collective-permute-start | bytes 786440 | tf_op jit(solution)/shard_map/ppermute | solution.py:18
  14.3 29.4 %collective-permute-start.5 = (bf16[256,512]{0,1:T(8,128)(2,1)S(1)}, bf16[256,512]{0,1:T(8,128)(2,1)}, u32[]{:S(2)}, u32[]{:S(2)}) collective-permute-start(bf16[256,512]{0,1:T(8,128)(2,1)S(1)} %copy.77), channel_id=1, source_target_pairs={{0,3},{1,4},{2,5},{3,6},{4,7},{5,8},{6,9},{7,10},{8,11},{9,12},{10... | collective-permute-start | bytes 786440 | tf_op jit(solution)/shard_map/ppermute | solution.py:18
  17.3 28.7 %collective-permute-start.6 = (bf16[256,512]{0,1:T(8,128)(2,1)S(1)}, bf16[256,512]{0,1:T(8,128)(2,1)}, u32[]{:S(2)}, u32[]{:S(2)}) collective-permute-start(bf16[256,512]{0,1:T(8,128)(2,1)S(1)} %copy.77), channel_id=1, source_target_pairs={{0,2},{1,3},{2,4},{3,5},{4,6},{5,7},{6,8},{7,9},{8,10},{9,11},{10,... | collective-permute-start | bytes 786440 | tf_op jit(solution)/shard_map/ppermute | solution.py:18
  21.8 29.2 %collective-permute-start.7 = (bf16[256,512]{0,1:T(8,128)(2,1)S(1)}, bf16[256,512]{0,1:T(8,128)(2,1)}, u32[]{:S(2)}, u32[]{:S(2)}) collective-permute-start(bf16[256,512]{0,1:T(8,128)(2,1)S(1)} %copy.77), channel_id=1, source_target_pairs={{0,1},{1,2},{2,3},{3,4},{4,5},{5,6},{6,7},{7,8},{8,9},{9,10},{10,1... | collective-permute-start | bytes 786440 | tf_op jit(solution)/shard_map/ppermute | solution.py:18
  25.0 27.1 %collective-permute-start = (bf16[256,512]{1,0:T(8,128)(2,1)}, bf16[256,512]{1,0:T(8,128)(2,1)}, u32[]{:S(2)}, u32[]{:S(2)}) collective-permute-start(bf16[256,512]{1,0:T(8,128)(2,1)} %param.18), channel_id=1, source_target_pairs={{0,4},{1,5},{2,6},{3,7},{4,8},{5,9},{6,10},{7,11},{8,12},{9,13},{1... | collective-permute-start | bytes 786440 | tf_op jit(solution)/shard_map/ppermute | solution.py:18
  34.0 19.9 %collective-permute-start.1 = (bf16[256,512]{1,0:T(8,128)(2,1)}, bf16[256,512]{1,0:T(8,128)(2,1)S(1)}, u32[]{:S(2)}, u32[]{:S(2)}) collective-permute-start(bf16[256,512]{1,0:T(8,128)(2,1)} %param.18), channel_id=1, source_target_pairs={{0,3},{1,4},{2,5},{3,6},{4,7},{5,8},{6,9},{7,10},{8,11},{9,12},{10... | collective-permute-start | bytes 786440 | tf_op jit(solution)/shard_map/ppermute | solution.py:18
  43.6 12.5 %copy-start.4 = (bf16[256,512]{1,0:T(8,128)(2,1)S(1)}, bf16[256,512]{1,0:T(8,128)(2,1)}, u32[]{:S(2)}) copy-start(bf16[256,512]{1,0:T(8,128)(2,1)} %param.18) | copy-start | bytes 786436
  43.6 11.0 %collective-permute-start.2 = (bf16[256,512]{1,0:T(8,128)(2,1)}, bf16[256,512]{1,0:T(8,128)(2,1)S(1)}, u32[]{:S(2)}, u32[]{:S(2)}) collective-permute-start(bf16[256,512]{1,0:T(8,128)(2,1)} %param.18), channel_id=1, source_target_pairs={{0,2},{1,3},{2,4},{3,5},{4,6},{5,7},{6,8},{7,9},{8,10},{9,11},{10,... | collective-permute-start | bytes 786440 | tf_op jit(solution)/shard_map/ppermute | solution.py:18
  46.1 9.3 %collective-permute-start.3 = (bf16[256,512]{1,0:T(8,128)(2,1)}, bf16[256,512]{1,0:T(8,128)(2,1)S(1)}, u32[]{:S(2)}, u32[]{:S(2)}) collective-permute-start(bf16[256,512]{1,0:T(8,128)(2,1)} %param.18), channel_id=1, source_target_pairs={{0,1},{1,2},{2,3},{3,4},{4,5},{5,6},{6,7},{7,8},{8,9},{9,10},{10,1... | collective-permute-start | bytes 786440 | tf_op jit(solution)/shard_map/ppermute | solution.py:18
  52.0 4.1 copy-start.6
  54.7 4.6 %copy-start.14 = (bf16[256,512]{1,0:T(8,128)(2,1)S(1)}, bf16[256,512]{1,0:T(8,128)(2,1)}, u32[]{:S(2)}) copy-start(bf16[256,512]{1,0:T(8,128)(2,1)} %param.16) | copy-start | bytes 786436
  70.9 0.7 copy-start.7
  70.9 299.1 %reduce-scatter.5.cloned.1.call-start = ((), (), s32[]{:S(2)}) async-start(), calls=%async_computation.7 | async-start | bytes 15728640 | tf_op jit(solution)/shard_map/reduce_scatter | solution.py:121
  90.8 50.3 %copy-start.9 = (f32[2048]{0:T(1024)S(1)}, f32[2048]{0:T(1024)}, u32[]{:S(2)}) copy-start(f32[2048]{0:T(1024)} %param.21) | copy-start | bytes 24580
  139.8 1.3 copy-start.3
  243.1 5.2 %copy-start.13 = (bf16[1,352,2048]{2,1,0:T(8,128)(2,1)S(1)}, bf16[1,352,2048]{2,1,0:T(8,128)(2,1)}, u32[]{:S(2)}) copy-start(bf16[1,352,2048]{2,1,0:T(8,128)(2,1)} %param.23) | copy-start | bytes 4325380
  254.7 0.7 copy-start.10
  254.8 0.7 copy-start.8
  254.8 1.3 copy-start.2
  254.8 167.5 %reduce-scatter.3.cloned.1.call-start = ((), (), s32[]{:S(2)}) async-start(), calls=%async_computation.6 | async-start | bytes 2621440 | tf_op jit(solution)/shard_map/reduce_scatter | solution.py:127
  256.4 4.5 %copy-start.12 = (bf16[704,2048]{1,0:T(8,128)(2,1)S(1)}, bf16[704,2048]{1,0:T(8,128)(2,1)}, u32[]{:S(2)}) copy-start(bf16[704,2048]{1,0:T(8,128)(2,1)} %param.25) | copy-start | bytes 8650756
  263.3 1.0 copy-start.5
  273.5 99.8 %all-to-all-start.2 = ((bf16[128,1,2,2,4,128]{5,4,3,2,1,0:T(4,128)(2,1)}), bf16[128,1,2,2,4,128]{5,4,3,2,1,0:T(4,128)(2,1)S(1)}, u32[]{:S(2)}, u32[]{:S(2)}) async-start(bf16[128,1,2,2,4,128]{5,4,3,2,1,0:T(4,128)(2,1)} %copy.93), calls=%async_computation.4 | async-start | bytes 1048576 | tf_op jit(solution)/shard_map/all_to_all | solution.py:170
  373.2 9.9 %copy-start.11 = (f32[256,4]{0,1:T(4,128)S(1)}, f32[256,4]{0,1:T(4,128)}, u32[]{:S(2)}) copy-start(f32[256,4]{0,1:T(4,128)} %param.28) | copy-start | bytes 12292
  373.3 33.5 %all-to-all-start.1 = ((bf16[32,48,512]{2,1,0:T(8,128)(2,1)}), bf16[32,48,512]{2,1,0:T(8,128)(2,1)S(1)}, u32[]{:S(2)}, u32[]{:S(2)}) async-start(bf16[32,48,512]{2,1,0:T(8,128)(2,1)} %bitcast.32), calls=%async_computation.3 | async-start | bytes 3145728 | tf_op jit(solution)/shard_map/all_to_all | solution.py:129
  416.2 8.1 %copy-start.1 = (bf16[1,2048,2,352]{1,3,2,0:T(8,128)(2,1)S(1)}, bf16[1,2048,2,352]{1,3,2,0:T(8,128)(2,1)}, u32[]{:S(2)}) copy-start(bf16[1,2048,2,352]{1,3,2,0:T(8,128)(2,1)} %param.22) | copy-start | bytes 8650756
Sparse Core Ops, SparseCore 0:
  71.0 66.4 all-reduce.2
  254.9 115.0 reduce-scatter.4
  372.5 46.0 reduce-scatter.2
where the time goes:
time: 432 us; the launch traced here: 431 us
  waiting for transfers between devices  159 us (37%)
  blocking collectives  83.4 us (19%)
  local copies, waits for them, and re-layouts  62.6 us (14%)
  starting transfers between devices  52.4 us (12%)
  matrix products  30.5 us (7%)
  other arithmetic  28.8 us (7%)
  between operations  14.3 us (3%)
    reduce_scatter x1, waiting for transfers between devices, per_device(): lax.psum_scatter(partial_value.reshape(EXPERTS * CAP, model_width), 'head...  92 us
    all_to_all x1, blocking collectives, per_device(): lax.all_to_all(outgoing, 'tok', split_axis=0, concat_axis=0, tiled=True)  83.4 us
    psum x1, waiting for transfers between devices, per_device(): total = lax.psum(projected, 'head')  46.8 us
    ppermute x8, starting transfers between devices, from_behind(): lax.ppermute(value, axis, [(source, source + steps) for source in range(l...  37.9 us
    all_to_all x1, waiting for transfers between devices, per_device(): lax.all_to_all(slot_cols.reshape(tok_count, local_experts * CAP, column_w...  20 us
    gather x1, local copies, waits for them, and re-layouts, per_device(): normed[source_row]  14.1 us
    unnamed x42, local copies, waits for them, and re-layouts  11.6 us
    all_to_all x1, starting transfers between devices, per_device(): lax.all_to_all(slot_cols.reshape(tok_count, local_experts * CAP, column_w...  9.84 us
  transfers between devices with their start and end apart: 13, of which 3 were waited for; matrix products, arithmetic and copies ran while one was open for 16% of the time, Pallas kernels for 0%

commit v1 on v0

--- a/solution.py
+++ b/solution.py
@@ -82,7 +82,8 @@
         .reshape(tok_rows, head_width)
     )
     projected = jnp.dot(attended, out_proj, preferred_element_type=jnp.float32)
-    total = lax.psum(projected, "head")
+    reply = jax.lax.all_gather(projected, "head")
+    total = jnp.sum(reply, axis=0)
     resid = hidden_in.astype(jnp.float32) + total
     mean_square = jnp.mean(resid * resid, axis=-1, keepdims=True)
     normed = (resid * lax.rsqrt(mean_square + 1e-06) * norm_gain).astype(jnp.bfloat16)

time: 432 us -> 471 us (1.090); the launches traced: 431 us -> 464 us
  waiting for transfers between devices: 159 us -> 181 us
  other arithmetic: 28.8 us -> 34.6 us
    all_gather x0 -> x1, waiting for transfers between devices: none -> 69.2 us  [per_device(): reply = jax.lax.all_gather(projected, 'head')]
    psum x1 -> x0, waiting for transfers between devices: 46.8 us -> none  [per_device(): total = lax.psum(projected, 'head')]
    reduce_sum x0 -> x1, other arithmetic: none -> 5.79 us  [per_device(): total = jnp.sum(reply, axis=0)]
  transfers between devices with their start and end apart: 13 -> 13, of which waited for: 3 -> 3; matrix products, arithmetic and copies ran while one was open for 16% -> 15% of each run, Pallas kernels for 0% -> 0%
where the time goes in v1:
time: 471 us; the launch traced here: 464 us
  waiting for transfers between devices  181 us (38%)
  blocking collectives  85.6 us (18%)
  local copies, waits for them, and re-layouts  62.8 us (13%)
  starting transfers between devices  54.1 us (11%)
  other arithmetic  34.6 us (7%)
  matrix products  30.6 us (6%)
  between operations  14.5 us (3%)
    reduce_scatter x1, waiting for transfers between devices, per_device(): lax.psum_scatter(partial_value.reshape(EXPERTS * CAP, model_width), 'head...  92 us
    all_to_all x1, blocking collectives, per_device(): lax.all_to_all(outgoing, 'tok', split_axis=0, concat_axis=0, tiled=True)  85.6 us
    all_gather x1, waiting for transfers between devices, per_device(): reply = jax.lax.all_gather(projected, 'head')  69.2 us
    ppermute x8, starting transfers between devices, from_behind(): lax.ppermute(value, axis, [(source, source + steps) for source in range(l...  37.9 us
    all_to_all x1, waiting for transfers between devices, per_device(): lax.all_to_all(slot_cols.reshape(tok_count, local_experts * CAP, column_w...  20 us
    gather x1, local copies, waits for them, and re-layouts, per_device(): normed[source_row]  14.1 us
    unnamed x42, local copies, waits for them, and re-layouts  11.6 us
    all_to_all x1, starting transfers between devices, per_device(): lax.all_to_all(slot_cols.reshape(tok_count, local_experts * CAP, column_w...  9.83 us
  transfers between devices with their start and end apart: 13, of which 3 were waited for; matrix products, arithmetic and copies ran while one was open for 15% of the time, Pallas kernels for 0%

profile of v1, /device:TPU:8, one launch (start us, length us, event | category | flops | bytes accessed | tf_op | source)
XLA Modules:
  0.0 463.5 jit_solution(4671012141818722594)
XLA Ops:
  8.5 5.8 %collective-permute-start.4 = (bf16[256,512]{0,1:T(8,128)(2,1)S(1)}, bf16[256,512]{0,1:T(8,128)(2,1)S(1)}, u32[]{:S(2)}, u32[]{:S(2)}) collective-permute-start(bf16[256,512]{0,1:T(8,128)(2,1)S(1)} %copy.77), channel_id=1, source_target_pairs={{0,4},{1,5},{2,6},{3,7},{4,8},{5,9},{6,10},{7,11},{8,12},{9,13},{1... | collective-permute-start | bytes 786440 | tf_op jit(solution)/shard_map/ppermute | solution.py:18
  14.3 3.1 collective-permute-start.5
  17.3 4.5 collective-permute-start.6
  21.8 3.1 collective-permute-start.7
  25.0 6.5 %collective-permute-start = (bf16[256,512]{1,0:T(8,128)(2,1)}, bf16[256,512]{1,0:T(8,128)(2,1)}, u32[]{:S(2)}, u32[]{:S(2)}) collective-permute-start(bf16[256,512]{1,0:T(8,128)(2,1)} %param.18), channel_id=1, source_target_pairs={{0,4},{1,5},{2,6},{3,7},{4,8},{5,9},{6,10},{7,11},{8,12},{9,13},{1... | collective-permute-start | bytes 786440 | tf_op jit(solution)/shard_map/ppermute | solution.py:18
  34.0 9.6 %collective-permute-start.1 = (bf16[256,512]{1,0:T(8,128)(2,1)}, bf16[256,512]{1,0:T(8,128)(2,1)S(1)}, u32[]{:S(2)}, u32[]{:S(2)}) collective-permute-start(bf16[256,512]{1,0:T(8,128)(2,1)} %param.18), channel_id=1, source_target_pairs={{0,3},{1,4},{2,5},{3,6},{4,7},{5,8},{6,9},{7,10},{8,11},{9,12},{10... | collective-permute-start | bytes 786440 | tf_op jit(solution)/shard_map/ppermute | solution.py:18
  46.1 4.0 collective-permute-start.3
  56.9 2.4 copy.76
  59.3 3.5 exponential_reduce_fusion
  62.8 4.5 fusion.15
  67.3 3.7 fusion.75
  72.1 9.0 %reduce-window.6 = s32[32,8,128]{2,1,0:T(8,128)S(1)} reduce-window(s32[32,8,128]{2,1,0:T(8,128)S(1)} %fusion.42, s32[]{:T(128)} %constant.46.clone.1), window={size=1x1x128 pad=0_0x0_0x127_0}, to_apply=%region_5.6 | reduce-window | flops 4161536 | bytes 262148 | tf_op jit(solution)/shard_map/reduce-window
  81.9 4.8 %scatter_custom_fusion.1 = s32[1536]{0:T(1024)S(1)} fusion(s32[1024]{0:T(1024)S(1)} %bitcast.160, s32[1024]{0:T(1024)S(1)} %add_select_fusion.3, s32[]{:T(128)} %constant.46.clone.1), kind=kCustom, calls=%fused_computation.98 | custom fusion | bytes 6148 | tf_op jit(solution)/shard_map/scatter | solution.py:109
  86.7 4.3 scatter_custom_fusion
  91.1 69.2 %all-gather.3.cloned.1.call-done = f32[1024,2048]{1,0:T(8,128)} async-done(((f32[256,2048]{1,0:T(8,128)}), f32[1024,2048]{1,0:T(8,128)}) %all-gather.3.cloned.1.call-update) | async-done | bytes 8388624 | tf_op jit(solution)/shard_map/all_gather | solution.py:85
  160.4 5.8 %reduce_sum.57 = f32[256,2048]{1,0:T(8,128)} reduce(f32[4,256,2048]{2,1,0:T(8,128)} %bitcast.148, f32[]{:T(128)} %constant.91.clone.1), dimensions={0}, to_apply=%region_2.3 | reduce | flops 1572864 | bytes 10485764 | tf_op jit(solution)/shard_map/reduce_sum | solution.py:86
  171.0 14.1 %gather_fusion = bf16[1536,2048]{1,0:T(8,128)(2,1)} fusion(bf16[256,2048]{1,0:T(8,128)(2,1)} %multiply_convert_fusion, s32[2048]{0:T(1024)S(1)} %pad_clamp_fusion), kind=kCustom, calls=%fused_computation | custom fusion | bytes 12589056 | tf_op jit(solution)/shard_map/gather | solution.py:112
  185.1 3.3 broadcast_select_fusion
  188.3 85.6 %all_to_all.15 = bf16[32,1,48,2048]{3,2,1,0:T(8,128)(2,1)S(1)} all-to-all(bf16[32,1,48,2048]{3,2,1,0:T(8,128)(2,1)S(1)} %broadcast_select_fusion), channel_id=1, replica_groups=mesh['head'=4,'tok'=32] {'tok'}, dimensions={0} | all-to-all | bytes 12582912 | tf_op jit(solution)/shard_map/all_to_all | solution.py:116
  273.9 5.2 %fusion.7 = f32[32,1,48,2,352]{4,2,3,0,1:T(8,128)S(1)} fusion(bf16[1,2048,2,352]{1,3,2,0:T(8,128)(2,1)S(1)} %copy-done, bf16[32,1,48,2048]{3,2,1,0:T(8,128)(2,1)S(1)} %all_to_all.15), kind=kOutput, calls=%fused_computation.22 | convolution fusion | flops 4429185024 | bytes 13500416 | tf_op jit(solution)/shard_map/secd,edgf->secgf/dot_general | solution.py:22
  279.1 6.4 %fusion.12 = f32[32,48,2048]{2,1,0:T(8,128)} fusion(bf16[1,352,2048]{2,1,0:T(8,128)(2,1)S(1)} %copy-done.13, f32[32,1,48,2,352]{4,2,3,0,1:T(8,128)S(1)} %fusion.7), kind=kOutput, calls=%fused_computation.28 | convolution fusion | flops 2217836544 | bytes 18350080 | tf_op jit(solution)/shard_map/secf,efd->secd/dot_general | solution.py:24
  287.2 4.5 fusion.18
  291.7 2.4 convolution_multiply_fusion
  296.0 4.3 scatter_custom_fusion.3
  304.2 6.2 %all-to-all-start.2 = ((bf16[128,1,2,2,4,128]{5,4,3,2,1,0:T(4,128)(2,1)}), bf16[128,1,2,2,4,128]{5,4,3,2,1,0:T(4,128)(2,1)S(1)}, u32[]{:S(2)}, u32[]{:S(2)}) async-start(bf16[128,1,2,2,4,128]{5,4,3,2,1,0:T(4,128)(2,1)} %copy.93), calls=%async_computation.4 | async-start | bytes 1048576 | tf_op jit(solution)/shard_map/all_to_all | solution.py:171
  310.4 92.0 %reduce-scatter.5.cloned.1.call-done = f32[1536,512]{1,0:T(8,128)} async-done(((f32[1536,2048]{1,0:T(8,128)}), f32[1536,512]{1,0:T(8,128)}) %reduce-scatter.5.cloned.1.call-update) | async-done | bytes 3145744 | tf_op jit(solution)/shard_map/reduce_scatter | solution.py:122
  402.5 3.2 convert_element_type.57
  405.7 9.8 %all-to-all-start.1 = ((bf16[32,48,512]{2,1,0:T(8,128)(2,1)}), bf16[32,48,512]{2,1,0:T(8,128)(2,1)S(1)}, u32[]{:S(2)}, u32[]{:S(2)}) async-start(bf16[32,48,512]{2,1,0:T(8,128)(2,1)} %bitcast.33), calls=%async_computation.3 | async-start | bytes 3145728 | tf_op jit(solution)/shard_map/all_to_all | solution.py:130
  419.2 20.0 %all-to-all-done.1 = bf16[32,48,512]{2,1,0:T(8,128)(2,1)S(1)} async-done(((bf16[32,48,512]{2,1,0:T(8,128)(2,1)}), bf16[32,48,512]{2,1,0:T(8,128)(2,1)S(1)}, u32[]{:S(2)}, u32[]{:S(2)}) %all-to-all-start.1) | async-done | bytes 1572896 | tf_op jit(solution)/shard_map/all_to_all | solution.py:130
  441.4 7.2 %gather_fusion.1 = f32[1024,512]{1,0:T(8,128)} fusion(f32[1536,512]{1,0:T(8,128)} %bitcast_convert_fusion, s32[1024]{0:T(1024)S(1)} %broadcast_clamp_fusion), kind=kCustom, calls=%fused_computation.1 | custom fusion | bytes 4198400 | tf_op jit(solution)/shard_map/gather | solution.py:137
  448.7 3.1 reshape.311
  451.8 2.9 multiply_reduce_fusion
  (117 shorter events, 34.9 us)
Async XLA Ops:
  7.2 266.7 %copy-start = (bf16[1,2048,2,352]{1,3,2,0:T(8,128)(2,1)S(1)}, bf16[1,2048,2,352]{1,3,2,0:T(8,128)(2,1)}, u32[]{:S(2)}) copy-start(bf16[1,2048,2,352]{1,3,2,0:T(8,128)(2,1)} %param.22) | copy-start | bytes 8650756
  7.2 153.2 %all-gather.3.cloned.1.call-start = ((), (), s32[]{:S(2)}) async-start(), calls=%async_computation.7 | async-start | bytes 10485760 | tf_op jit(solution)/shard_map/all_gather | solution.py:85
  8.5 25.6 %collective-permute-start.4 = (bf16[256,512]{0,1:T(8,128)(2,1)S(1)}, bf16[256,512]{0,1:T(8,128)(2,1)S(1)}, u32[]{:S(2)}, u32[]{:S(2)}) collective-permute-start(bf16[256,512]{0,1:T(8,128)(2,1)S(1)} %copy.77), channel_id=1, source_target_pairs={{0,4},{1,5},{2,6},{3,7},{4,8},{5,9},{6,10},{7,11},{8,12},{9,13},{1... | collective-permute-start | bytes 786440 | tf_op jit(solution)/shard_map/ppermute | solution.py:18
  14.3 29.4 %collective-permute-start.5 = (bf16[256,512]{0,1:T(8,128)(2,1)S(1)}, bf16[256,512]{0,1:T(8,128)(2,1)}, u32[]{:S(2)}, u32[]{:S(2)}) collective-permute-start(bf16[256,512]{0,1:T(8,128)(2,1)S(1)} %copy.77), channel_id=1, source_target_pairs={{0,3},{1,4},{2,5},{3,6},{4,7},{5,8},{6,9},{7,10},{8,11},{9,12},{10... | collective-permute-start | bytes 786440 | tf_op jit(solution)/shard_map/ppermute | solution.py:18
  17.3 28.7 %collective-permute-start.6 = (bf16[256,512]{0,1:T(8,128)(2,1)S(1)}, bf16[256,512]{0,1:T(8,128)(2,1)}, u32[]{:S(2)}, u32[]{:S(2)}) collective-permute-start(bf16[256,512]{0,1:T(8,128)(2,1)S(1)} %copy.77), channel_id=1, source_target_pairs={{0,2},{1,3},{2,4},{3,5},{4,6},{5,7},{6,8},{7,9},{8,10},{9,11},{10,... | collective-permute-start | bytes 786440 | tf_op jit(solution)/shard_map/ppermute | solution.py:18
  21.8 29.2 %collective-permute-start.7 = (bf16[256,512]{0,1:T(8,128)(2,1)S(1)}, bf16[256,512]{0,1:T(8,128)(2,1)}, u32[]{:S(2)}, u32[]{:S(2)}) collective-permute-start(bf16[256,512]{0,1:T(8,128)(2,1)S(1)} %copy.77), channel_id=1, source_target_pairs={{0,1},{1,2},{2,3},{3,4},{4,5},{5,6},{6,7},{7,8},{8,9},{9,10},{10,1... | collective-permute-start | bytes 786440 | tf_op jit(solution)/shard_map/ppermute | solution.py:18
  25.0 27.1 %collective-permute-start = (bf16[256,512]{1,0:T(8,128)(2,1)}, bf16[256,512]{1,0:T(8,128)(2,1)}, u32[]{:S(2)}, u32[]{:S(2)}) collective-permute-start(bf16[256,512]{1,0:T(8,128)(2,1)} %param.18), channel_id=1, source_target_pairs={{0,4},{1,5},{2,6},{3,7},{4,8},{5,9},{6,10},{7,11},{8,12},{9,13},{1... | collective-permute-start | bytes 786440 | tf_op jit(solution)/shard_map/ppermute | solution.py:18
  34.0 19.9 %collective-permute-start.1 = (bf16[256,512]{1,0:T(8,128)(2,1)}, bf16[256,512]{1,0:T(8,128)(2,1)S(1)}, u32[]{:S(2)}, u32[]{:S(2)}) collective-permute-start(bf16[256,512]{1,0:T(8,128)(2,1)} %param.18), channel_id=1, source_target_pairs={{0,3},{1,4},{2,5},{3,6},{4,7},{5,8},{6,9},{7,10},{8,11},{9,12},{10... | collective-permute-start | bytes 786440 | tf_op jit(solution)/shard_map/ppermute | solution.py:18
  43.6 12.5 %copy-start.4 = (bf16[256,512]{1,0:T(8,128)(2,1)S(1)}, bf16[256,512]{1,0:T(8,128)(2,1)}, u32[]{:S(2)}) copy-start(bf16[256,512]{1,0:T(8,128)(2,1)} %param.18) | copy-start | bytes 786436
  43.6 11.0 %collective-permute-start.2 = (bf16[256,512]{1,0:T(8,128)(2,1)}, bf16[256,512]{1,0:T(8,128)(2,1)S(1)}, u32[]{:S(2)}, u32[]{:S(2)}) collective-permute-start(bf16[256,512]{1,0:T(8,128)(2,1)} %param.18), channel_id=1, source_target_pairs={{0,2},{1,3},{2,4},{3,5},{4,6},{5,7},{6,8},{7,9},{8,10},{9,11},{10,... | collective-permute-start | bytes 786440 | tf_op jit(solution)/shard_map/ppermute | solution.py:18
  46.1 9.3 %collective-permute-start.3 = (bf16[256,512]{1,0:T(8,128)(2,1)}, bf16[256,512]{1,0:T(8,128)(2,1)S(1)}, u32[]{:S(2)}, u32[]{:S(2)}) collective-permute-start(bf16[256,512]{1,0:T(8,128)(2,1)} %param.18), channel_id=1, source_target_pairs={{0,1},{1,2},{2,3},{3,4},{4,5},{5,6},{6,7},{7,8},{8,9},{9,10},{10,1... | collective-permute-start | bytes 786440 | tf_op jit(solution)/shard_map/ppermute | solution.py:18
  52.0 4.1 copy-start.6
  54.7 4.6 copy-start.14
  71.0 0.7 copy-start.7
  71.0 331.5 %reduce-scatter.5.cloned.1.call-start = ((), (), s32[]{:S(2)}) async-start(), calls=%async_computation.6 | async-start | bytes 15728640 | tf_op jit(solution)/shard_map/reduce_scatter | solution.py:122
  166.1 3.5 copy-start.9
  168.4 1.3 copy-start.3
  273.9 5.2 %copy-start.13 = (bf16[1,352,2048]{2,1,0:T(8,128)(2,1)S(1)}, bf16[1,352,2048]{2,1,0:T(8,128)(2,1)}, u32[]{:S(2)}) copy-start(bf16[1,352,2048]{2,1,0:T(8,128)(2,1)} %param.23) | copy-start | bytes 4325380
  285.5 0.7 copy-start.10
  285.5 0.7 copy-start.8
  285.6 1.3 copy-start.2
  285.6 169.2 %reduce-scatter.3.cloned.1.call-start = ((), (), s32[]{:S(2)}) async-start(), calls=%async_computation.5 | async-start | bytes 2621440 | tf_op jit(solution)/shard_map/reduce_scatter | solution.py:128
  287.2 4.5 copy-start.12
  294.1 1.0 copy-start.5
  304.2 101.5 %all-to-all-start.2 = ((bf16[128,1,2,2,4,128]{5,4,3,2,1,0:T(4,128)(2,1)}), bf16[128,1,2,2,4,128]{5,4,3,2,1,0:T(4,128)(2,1)S(1)}, u32[]{:S(2)}, u32[]{:S(2)}) async-start(bf16[128,1,2,2,4,128]{5,4,3,2,1,0:T(4,128)(2,1)} %copy.93), calls=%async_computation.4 | async-start | bytes 1048576 | tf_op jit(solution)/shard_map/all_to_all | solution.py:171
  405.7 9.8 %copy-start.11 = (f32[256,4]{0,1:T(4,128)S(1)}, f32[256,4]{0,1:T(4,128)}, u32[]{:S(2)}) copy-start(f32[256,4]{0,1:T(4,128)} %param.28) | copy-start | bytes 12292
  405.7 33.5 %all-to-all-start.1 = ((bf16[32,48,512]{2,1,0:T(8,128)(2,1)}), bf16[32,48,512]{2,1,0:T(8,128)(2,1)S(1)}, u32[]{:S(2)}, u32[]{:S(2)}) async-start(bf16[32,48,512]{2,1,0:T(8,128)(2,1)} %bitcast.33), calls=%async_computation.3 | async-start | bytes 3145728 | tf_op jit(solution)/shard_map/all_to_all | solution.py:130
  448.7 8.1 %copy-start.1 = (bf16[1,2048,2,352]{1,3,2,0:T(8,128)(2,1)S(1)}, bf16[1,2048,2,352]{1,3,2,0:T(8,128)(2,1)}, u32[]{:S(2)}) copy-start(bf16[1,2048,2,352]{1,3,2,0:T(8,128)(2,1)} %param.22) | copy-start | bytes 8650756
Sparse Core Ops, SparseCore 0:
  71.1 89.1 all-gather.2
  285.7 116.7 reduce-scatter.4
  404.9 46.0 reduce-scatter.2
